TPU v7x, 32 devices: a whole 2x2x4 slice. The times are simulated.
32 devices in a mesh: row: 8 (over y, x, core), col: 4 (over z).
Axes of the slice: x: 2, y: 2, z: 4, core: 2. Of those that a mesh axis runs over, the one named last changes fastest.
Arguments:
- diag_factor: float32 [1024, 1024], P('row', 'col'), may hold values from -1 to 2.5, as said below
- panel_factor: float32 [4096, 1024], P('row', 'col'), may hold values from -0.09375 to 0.09375
- left_factor: float32 [4096, 2048], P('row', 'col'), may hold values from -0.09375 to 0.09375
- pivot_factor: float32 [1024, 2048], P('row', 'col'), may hold values from -0.1875 to 0.1875
- panel_adjoint: float32 [4096, 1024], P('row', 'col'), may hold values from -6 to 6
- left_adjoint: float32 [4096, 2048], P('row', 'col'), may hold values from -6 to 6
- pivot_adjoint: float32 [1024, 2048], P('row', 'col'), may hold values from -6 to 6
- diag_adjoint: float32 [1024, 1024], P('row', 'col'), may hold values from -6 to 6
Outputs:
- solved_panel: float32 [4096, 1024], P('row', 'col')
- left_out: float32 [4096, 2048], P('row', 'col')
- pivot_out: float32 [1024, 2048], P('row', 'col')
- diag_out: float32 [1024, 1024], P('row', 'col')
Inputs may be any that keep to these rules, and one draw needn't show every extreme that they name: diag_factor is lower triangular: zero above the diagonal, diagonal entries at least 1.
All inputs are finite; a program needn't handle non-finite values.
Results may differ from a plain program's by a relative error of at most 0.000073.
Values sent between devices are 32-bit elements; how exact they have to be, the bound alone decides.
No kernel may reach another device: no remote copies, remote signals or barrier semaphores. Data moves between devices by JAX's collectives and lax.ppermute only.
A program may use at most 64 MiB of HBM per device.

v0:
```python
import jax
import jax.numpy as jnp
from jax import lax
from jax.sharding import PartitionSpec as P


def right_solve(tile, source):
    return jax.scipy.linalg.solve_triangular(tile, source.T, trans="T", lower=True).T


def local(
    diag_factor,
    panel_factor,
    left_factor,
    pivot_factor,
    panel_adjoint,
    left_adjoint,
    pivot_adjoint,
    diag_adjoint,
):
    highest = lax.Precision.HIGHEST
    block_width = panel_adjoint.shape[1]
    my_col = lax.axis_index("col")
    my_row = lax.axis_index("row")
    column_block = lax.all_gather(diag_factor, "row", axis=0, tiled=True)
    whole_diag = lax.all_gather(column_block, "col", axis=1, tiled=True)
    full_rows = lax.all_gather(panel_adjoint, "col", axis=1, tiled=True)
    solved = right_solve(whole_diag, full_rows)
    solved_panel = lax.dynamic_slice_in_dim(solved, my_col * block_width, block_width, 1)
    picked = solved
    left_out = left_adjoint - jnp.dot(
        picked,
        lax.all_gather(pivot_factor, "row", axis=0, tiled=True),
        precision=highest,
        preferred_element_type=jnp.float32,
    )
    own_rows = diag_adjoint.shape[0]
    picked = solved
    square = jnp.einsum("rk,rc->kc", picked, panel_factor, precision=highest)
    pivot_part = jnp.einsum("rk,rc->kc", picked, left_factor, precision=highest)
    summed = lax.psum_scatter(
        jnp.concatenate([square, pivot_part], axis=1), "row", scatter_dimension=0, tiled=True
    )
    square_sum = summed[:, :block_width]
    pivot_sum = summed[:, block_width:]
    pivot_out = pivot_adjoint - pivot_sum
    global_row = my_row * own_rows + lax.broadcasted_iota(jnp.int32, (own_rows, block_width), 0)
    global_col = my_col * block_width + lax.broadcasted_iota(jnp.int32, (own_rows, block_width), 1)
    diag_out = diag_adjoint - jnp.where(global_col <= global_row, square_sum, 0.0)
    return (solved_panel, left_out, pivot_out, diag_out)


def solution(mesh):
    in_specs = (
        P("row", "col"),
        P("row", "col"),
        P("row", "col"),
        P("row", "col"),
        P("row", "col"),
        P("row", "col"),
        P("row", "col"),
        P("row", "col"),
    )
    out_specs = (P("row", "col"), P("row", "col"), P("row", "col"), P("row", "col"))
    return jax.shard_map(local, mesh=mesh, in_specs=in_specs, out_specs=out_specs, check_vma=False)
```

profile of v0, /device:TPU:0, one launch (start us, length us, event | category | flops | bytes accessed | tf_op | source)
XLA Modules:
  0.0 313.2 jit_solution(5399329404083906748)
XLA Ops:
  7.2 0.7 all-gather.5.cloned.1.call-update
  7.9 0.0 all-gather.7.cloned.1.call-start
  8.0 28.0 %all-gather.5.cloned.1.call-done = f32[1024,256]{1,0:T(8,128)} async-done(((f32[128,256]{1,0:T(8,128)}), f32[1024,256]{1,0:T(8,128)}) %all-gather.5.cloned.1.call-update) | async-done | bytes 1048592 | tf_op jit(solution)/shard_map/all_gather | solution.py:25
  36.0 0.0 all-gather.9.cloned.1.call-start
  36.1 0.7 all-gather.9.cloned.1.call-update
  36.8 0.0 all-gather.11.cloned.1.call-start
  36.8 0.5 all-gather.11.cloned.1.call-update
  37.3 0.0 reduce-scatter.2.cloned.1.call-start
  37.4 80.9 %all-gather.7.cloned.1.call-done = f32[1024,1024]{1,0:T(8,128)} async-done(((f32[1024,256]{1,0:T(8,128)}), f32[1024,1024]{1,0:T(8,128)}) %all-gather.7.cloned.1.call-update) | async-done | bytes 4194320 | tf_op jit(solution)/shard_map/all_gather | solution.py:26
  118.3 4.8 %fusion = f32[1024,1024]{1,0:T(8,128)} fusion(f32[1024,1024]{1,0:T(8,128)} %all-gather.7.cloned.1.call-done), kind=kLoop, calls=%fused_computation.3 | loop fusion | flops 2097152 | bytes 8388608 | tf_op jit(solution)/shard_map/jit(_solve_triangular)/triangular_solve | solution.py:8
  123.1 23.2 %while.1 = (s32[]{:T(128)}, f32[1024,1024]{1,0:T(8,128)}, s32[8,2]{0,1:T(2,128)S(1)}, f32[8,128,128]{2,1,0:T(8,128)S(1)}, s32[]{:T(128)}) while((s32[]{:T(128)}, f32[1024,1024]{1,0:T(8,128)}, s32[8,2]{0,1:T(2,128)S(1)}, f32[8,128,128]{2,1,0:T(8,128)S(1)}, s32[]{:T(128)}) %tuple.27), condition=%wide.while_cond, body=%wide.while_body.sunk | while | flops 2 | bytes 131181 | solution.py:8
  123.1 0.1 constant_dynamic-slice_fusion.2
  123.2 0.5 fusion.56
  123.7 2.3 bitcast_dynamic-update-slice_fusion.2
  126.0 0.1 constant_dynamic-slice_fusion.2
  126.1 0.5 fusion.56
  126.6 2.3 bitcast_dynamic-update-slice_fusion.2
  128.9 0.1 constant_dynamic-slice_fusion.2
  129.0 0.5 fusion.56
  129.5 2.3 bitcast_dynamic-update-slice_fusion.2
  131.8 0.1 constant_dynamic-slice_fusion.2
  131.9 0.5 fusion.56
  132.4 2.3 bitcast_dynamic-update-slice_fusion.2
  134.8 0.1 constant_dynamic-slice_fusion.2
  134.8 0.5 fusion.56
  135.3 2.3 bitcast_dynamic-update-slice_fusion.2
  137.7 0.1 constant_dynamic-slice_fusion.2
  137.7 0.5 fusion.56
  138.3 2.3 bitcast_dynamic-update-slice_fusion.2
  140.6 0.1 constant_dynamic-slice_fusion.2
  140.6 0.5 fusion.56
  141.2 2.3 bitcast_dynamic-update-slice_fusion.2
  143.5 0.1 constant_dynamic-slice_fusion.2
  143.6 0.5 fusion.56
  144.1 2.2 bitcast_dynamic-update-slice_fusion.2
  146.3 78.8 %custom-call.4 = f32[8,128,128]{1,2,0:T(8,128)S(1)} custom-call(f32[8,128,128]{2,1,0:T(8,128)S(1)} %get-tuple-element.11), custom_call_target="InvertDiagBlocksLowerTriangular" | custom-call | tf_op jit(solution)/shard_map/jit(_solve_triangular)/triangular_solve | solution.py:8
  225.2 1.5 fusion.19
  226.7 1.6 convolution_subtract_fusion.4
  228.3 0.4 fusion.26
  228.7 2.0 convolution_subtract_fusion.3
  230.7 0.4 fusion.27
  231.1 2.4 convolution_subtract_fusion.6
  233.5 0.4 fusion.28
  233.9 2.8 convolution_subtract_fusion.7
  236.6 0.4 constant_dynamic-update-slice_fusion.4
  237.1 3.2 %convolution_subtract_fusion.2 = f32[128,512]{0,1:T(8,128)S(1)} fusion(f32[640,512]{1,0:T(8,128)S(1)} %constant_dynamic-update-slice_fusion, f32[1024,1024]{1,0:T(8,128)} %get-tuple-element.83, f32[1024,512]{0,1:T(8,128)S(1)} %bitcast.65), kind=kOutput, calls=%fused_computation.8 | convolution fusion | flops 503382016 | bytes 2162688 | tf_op jit(solution)/shard_map/jit(_solve_triangular)/triangular_solve | solution.py:8
  240.3 0.4 constant_dynamic-update-slice_fusion.10
  240.9 3.6 %convolution_subtract_fusion.5 = f32[128,512]{0,1:T(8,128)S(1)} fusion(f32[768,512]{1,0:T(8,128)S(1)} %constant_dynamic-update-slice_fusion.5, f32[1024,1024]{1,0:T(8,128)} %get-tuple-element.83, f32[1024,512]{0,1:T(8,128)S(1)} %bitcast.66), kind=kOutput, calls=%fused_computation.11 | convolution fusion | flops 604045312 | bytes 2490368 | tf_op jit(solution)/shard_map/jit(_solve_triangular)/triangular_solve | solution.py:8
  244.5 0.4 constant_dynamic-update-slice_fusion.17
  245.0 4.3 %convolution_subtract_fusion.1 = f32[128,512]{0,1:T(8,128)S(1)} fusion(f32[896,512]{1,0:T(8,128)S(1)} %constant_dynamic-update-slice_fusion.11, f32[1024,1024]{1,0:T(8,128)} %get-tuple-element.83, f32[1024,512]{0,1:T(8,128)S(1)} %bitcast.67), kind=kOutput, calls=%fused_computation.7 | convolution fusion | flops 704708608 | bytes 2818048 | tf_op jit(solution)/shard_map/jit(_solve_triangular)/triangular_solve | solution.py:8
  249.4 1.3 convolution_dynamic-update-slice_fusion
  250.8 2.0 fusion.36
  252.9 3.5 %fusion.37 = f32[1024,512]{0,1:T(8,128)S(1)} fusion(f32[1024,512]{1,0:T(8,128)S(1)} %constant_dynamic-update-slice_fusion.18, f32[512,512]{1,0:T(8,128)S(1)} %copy-done), kind=kOutput, calls=%fused_computation.89 | convolution fusion | flops 3221225472 | bytes 5242880 | tf_op jit(solution)/shard_map/rk,rc->kc/dot_general | solution.py:40
  256.4 2.0 pad_maximum_fusion
  258.5 1.1 copy.12
  259.5 1.0 copy.13
  260.6 0.8 dynamic-slice_bitcast_fusion
  261.4 2.1 copy.14
  263.5 6.6 %convolution_subtract_fusion = f32[512,512]{1,0:T(8,128)} fusion(f32[512,512]{1,0:T(8,128)} %param.13, f32[1024,512]{1,0:T(8,128)S(1)} %constant_dynamic-update-slice_fusion.18, f32[1024,512]{1,0:T(8,128)} %all-gather.11.cloned.1.call-done), kind=kOutput, calls=%fused_computation.5 | convolution fusion | flops 3221487616 | bytes 6291456 | tf_op jit(solution)/shard_map/dot_general | solution.py:31
  270.1 33.0 %reduce-scatter.2.cloned.1.call-done = f32[128,768]{0,1:T(8,128)} async-done(((f32[1024,768]{0,1:T(8,128)}), f32[128,768]{0,1:T(8,128)}) %reduce-scatter.2.cloned.1.call-update) | async-done | bytes 393232 | tf_op jit(solution)/shard_map/reduce_scatter | solution.py:41
  303.1 1.0 slice_subtract_fusion
  304.1 0.8 copy.15
  304.9 1.0 fusion.23
  305.9 0.8 copy.16
  (40 shorter events, 0.6 us)
Async XLA Ops:
  7.2 245.7 %copy-start = (f32[512,512]{1,0:T(8,128)S(1)}, f32[512,512]{1,0:T(8,128)}, u32[]{:S(2)}) copy-start(f32[512,512]{1,0:T(8,128)} %param.10) | copy-start | bytes 3145732
  7.2 28.8 %all-gather.5.cloned.1.call-start = ((), (), s32[]{:S(2)}) async-start(), calls=%async_computation.1 | async-start | bytes 1179648 | tf_op jit(solution)/shard_map/all_gather | solution.py:25
  7.9 110.4 %all-gather.7.cloned.1.call-start = ((), (), s32[]{:S(2)}) async-start(), calls=%async_computation.2 | async-start | bytes 5242880 | tf_op jit(solution)/shard_map/all_gather | solution.py:26
  36.0 189.1 %all-gather.9.cloned.1.call-start = ((), (), s32[]{:S(2)}) async-start(), calls=%async_computation.3 | async-start | bytes 2621440 | tf_op jit(solution)/shard_map/all_gather | solution.py:27
  36.8 226.7 %all-gather.11.cloned.1.call-start = ((), (), s32[]{:S(2)}) async-start(), calls=%async_computation.4 | async-start | bytes 2359296 | tf_op jit(solution)/shard_map/all_gather | solution.py:33
  37.3 265.8 %reduce-scatter.2.cloned.1.call-start = ((), (), s32[]{:S(2)}) async-start(), calls=%async_computation.5 | async-start | bytes 3538944 | tf_op jit(solution)/shard_map/reduce_scatter | solution.py:41
  225.1 19.4 %copy-start.3 = (f32[8,128,128]{1,2,0:T(8,128)}, f32[8,128,128]{1,2,0:T(8,128)S(1)}, u32[]{:S(2)}) copy-start(f32[8,128,128]{1,2,0:T(8,128)S(1)} %custom-call.4) | copy-start | bytes 1572868
  225.1 5.9 %copy-start.1 = (f32[512,1024]{1,0:T(8,128)S(1)}, f32[512,1024]{1,0:T(8,128)}, u32[]{:S(2)}) copy-start(f32[512,1024]{1,0:T(8,128)} %all-gather.9.cloned.1.call-done) | copy-start | bytes 6291460
  249.4 1.5 copy-start.2
Sparse Core Ops, SparseCore 0:
  9.9 26.0 all-gather.4
  37.6 80.7 all-gather.6
  119.9 44.1 all-gather.8
  165.9 26.7 all-gather.10
  258.6 44.4 reduce-scatter.1
where the time goes:
time: 314 us; the launch traced here: 313 us
  waiting for transfers between devices  144 us (46%)
  other arithmetic  87.5 us (28%)
  matrix products  37.1 us (12%)
  local copies, waits for them, and re-layouts  30.1 us (10%)
  between operations  14.2 us (5%)
    another operation x3, other arithmetic, right_solve(): jax.scipy.linalg.solve_triangular(tile, source.T, trans='T', lower=True)  83.5 us
    all_gather x1, waiting for transfers between devices, local(): whole_diag = lax.all_gather(column_block, 'col', axis=1, tiled=True)  80.9 us
    reduce_scatter x1, waiting for transfers between devices, local(): lax.psum_scatter(jnp.concatenate([square, pivot_part], axis=1), 'row', sc...  33 us
    all_gather x1, waiting for transfers between devices, local(): column_block = lax.all_gather(diag_factor, 'row', axis=0, tiled=True)  28 us
    another operation x15, matrix products, right_solve(): jax.scipy.linalg.solve_triangular(tile, source.T, trans='T', lower=True)  24.9 us
    another operation x24, local copies, waits for them, and re-layouts  23.1 us
    dot_general x1, matrix products, local(): jnp.dot(picked, lax.all_gather(pivot_factor, 'row', axis=0, tiled=True),...  6.61 us
  transfers between devices with their start and end apart: 5, of which 3 were waited for; matrix products, arithmetic and copies ran while one was open for 48% of the time, Pallas kernels for 0%

commit v1 on v0

--- a/solution.py
+++ b/solution.py
@@ -23,7 +23,12 @@
     my_col = lax.axis_index("col")
     my_row = lax.axis_index("row")
     column_block = lax.all_gather(diag_factor, "row", axis=0, tiled=True)
-    whole_diag = lax.all_gather(column_block, "col", axis=1, tiled=True)
+    ring = [column_block]
+    for hop in range(3):
+        ring.append(lax.ppermute(ring[-1], "col", [(dev, (dev + 1) % 4) for dev in range(4)]))
+    whole_diag = jnp.roll(
+        jnp.concatenate(ring[::-1], axis=1), (lax.axis_index("col") + 1) * ring[0].shape[1], axis=1
+    )
     full_rows = lax.all_gather(panel_adjoint, "col", axis=1, tiled=True)
     solved = right_solve(whole_diag, full_rows)
     solved_panel = lax.dynamic_slice_in_dim(solved, my_col * block_width, block_width, 1)

time: 314 us -> 348 us (1.11)
  starting transfers between devices: 0.19 us -> 15.1 us
  waiting for transfers between devices: 144 us -> 155 us
  local copies, waits for them, and re-layouts: 30.1 us -> 39.7 us
    ppermute x0 -> x3, waiting for transfers between devices: none -> 94.4 us  [local(): lax.ppermute(ring[-1], 'col', [(dev, (dev + 1) % 4) for dev in range(4)])]
    all_gather x1 -> x0, waiting for transfers between devices: 80.9 us -> none  [local(): whole_diag = lax.all_gather(column_block, 'col', axis=1, tiled=True)]
    ppermute x0 -> x3, starting transfers between devices: none -> 14.9 us  [local(): lax.ppermute(ring[-1], 'col', [(dev, (dev + 1) % 4) for dev in range(4)])]
    another operation x24, local copies, waits for them, and re-layouts: 23.1 us -> 28.1 us
    unnamed x31 -> x40, local copies, waits for them, and re-layouts: 6.11 us -> 10.5 us
  transfers between devices with their start and end apart: 5 -> 7, of which waited for: 3 -> 5; matrix products, arithmetic and copies ran while one was open for 48% -> 46% of each run, Pallas kernels for 0% -> 0%
where the time goes in v1:
time: 348 us; the launch traced here: 347 us
  waiting for transfers between devices  155 us (45%)
  other arithmetic  86 us (25%)
  local copies, waits for them, and re-layouts  39.7 us (11%)
  matrix products  37 us (11%)
  starting transfers between devices  15.1 us (4%)
  between operations  14.3 us (4%)
    ppermute x3, waiting for transfers between devices, local(): lax.ppermute(ring[-1], 'col', [(dev, (dev + 1) % 4) for dev in range(4)])  94.4 us
    another operation x3, other arithmetic, right_solve(): jax.scipy.linalg.solve_triangular(tile, source.T, trans='T', lower=True)  82 us
    reduce_scatter x1, waiting for transfers between devices, local(): lax.psum_scatter(jnp.concatenate([square, pivot_part], axis=1), 'row', sc...  32 us
    another operation x24, local copies, waits for them, and re-layouts  28.1 us
    all_gather x1, waiting for transfers between devices, local(): column_block = lax.all_gather(diag_factor, 'row', axis=0, tiled=True)  27.3 us
    another operation x15, matrix products, right_solve(): jax.scipy.linalg.solve_triangular(tile, source.T, trans='T', lower=True)  24.9 us
    ppermute x3, starting transfers between devices, local(): lax.ppermute(ring[-1], 'col', [(dev, (dev + 1) % 4) for dev in range(4)])  14.9 us
    unnamed x40, local copies, waits for them, and re-layouts  10.5 us
  transfers between devices with their start and end apart: 7, of which 5 were waited for; matrix products, arithmetic and copies ran while one was open for 46% of the time, Pallas kernels for 0%

profile of v1, /device:TPU:0, one launch (start us, length us, event | category | flops | bytes accessed | tf_op | source)
XLA Modules:
  0.0 347.1 jit_solution(8311891098712543989)
XLA Ops:
  7.2 0.7 all-gather.4.cloned.1.call-update
  8.0 0.7 all-gather.6.cloned.1.call-update
  8.7 27.3 %all-gather.4.cloned.1.call-done = f32[1024,256]{1,0:T(8,128)} async-done(((f32[128,256]{1,0:T(8,128)}), f32[1024,256]{1,0:T(8,128)}) %all-gather.4.cloned.1.call-update) | async-done | bytes 1048592 | tf_op jit(solution)/shard_map/all_gather | solution.py:25
  36.0 1.5 collective-permute-start
  37.5 40.1 %collective-permute-done = f32[1024,256]{1,0:T(8,128)S(1)} collective-permute-done((f32[1024,256]{1,0:T(8,128)}, f32[1024,256]{1,0:T(8,128)S(1)}, u32[]{:S(2)}, u32[]{:S(2)}) %collective-permute-start) | collective-permute-done | bytes 1048608 | tf_op jit(solution)/shard_map/ppermute | solution.py:28
  77.6 13.4 %collective-permute-start.1 = (f32[1024,256]{1,0:T(8,128)S(1)}, f32[1024,256]{1,0:T(8,128)S(1)}, u32[]{:S(2)}, u32[]{:S(2)}) collective-permute-start(f32[1024,256]{1,0:T(8,128)S(1)} %collective-permute-done), channel_id=1, source_target_pairs={{0,1},{1,2},{2,3},{3,0},{4,5},{5,6},{6,7},{7,4},{8,9},{9,10},{10,1... | collective-permute-start | bytes 3145736 | tf_op jit(solution)/shard_map/ppermute | solution.py:28
  91.0 28.8 %collective-permute-done.1 = f32[1024,256]{1,0:T(8,128)S(1)} collective-permute-done((f32[1024,256]{1,0:T(8,128)S(1)}, f32[1024,256]{1,0:T(8,128)S(1)}, u32[]{:S(2)}, u32[]{:S(2)}) %collective-permute-start.1) | collective-permute-done | bytes 1048608 | tf_op jit(solution)/shard_map/ppermute | solution.py:28
  119.9 25.5 %collective-permute-done.2 = f32[1024,256]{1,0:T(8,128)} collective-permute-done((f32[1024,256]{1,0:T(8,128)S(1)}, f32[1024,256]{1,0:T(8,128)}, u32[]{:S(2)}, u32[]{:S(2)}) %collective-permute-start.2) | collective-permute-done | bytes 1048608 | tf_op jit(solution)/shard_map/ppermute | solution.py:28
  145.4 1.4 constant_dynamic-update-slice_fusion.7
  146.8 0.1 constant_dynamic-update-slice_fusion.6
  147.0 0.2 constant_dynamic-update-slice_fusion.5
  147.1 0.9 copy-done.1
  148.1 0.1 constant_dynamic-update-slice_fusion.4
  148.2 1.4 constant_dynamic-update-slice_fusion.3
  149.6 0.2 constant_dynamic-update-slice_fusion.2
  149.8 0.2 constant_dynamic-update-slice_fusion.1
  149.9 0.2 constant_dynamic-update-slice_fusion
  150.1 2.4 dynamic-slice_select_fusion
  152.5 28.1 %while.1 = (s32[]{:T(128)}, f32[1024,1024]{1,0:T(8,128)}, s32[8,2]{0,1:T(2,128)S(1)}, f32[8,128,128]{2,1,0:T(8,128)}, s32[]{:T(128)}) while((s32[]{:T(128)}, f32[1024,1024]{1,0:T(8,128)}, s32[8,2]{0,1:T(2,128)S(1)}, f32[8,128,128]{2,1,0:T(8,128)}, s32[]{:T(128)}) %tuple.27), condition=%wide.while_cond, body=%wide.while_body.sunk | while | flops 2 | bytes 132705 | solution.py:8
  152.6 0.5 fusion.55
  153.1 2.9 bitcast_dynamic-update-slice_fusion.2
  156.1 0.5 fusion.55
  156.6 2.9 bitcast_dynamic-update-slice_fusion.2
  159.6 0.5 fusion.55
  160.1 2.9 bitcast_dynamic-update-slice_fusion.2
  163.1 0.5 fusion.55
  163.7 2.9 bitcast_dynamic-update-slice_fusion.2
  166.7 0.5 fusion.55
  167.2 2.9 bitcast_dynamic-update-slice_fusion.2
  170.2 0.5 fusion.55
  170.7 2.9 bitcast_dynamic-update-slice_fusion.2
  173.7 0.5 fusion.55
  174.2 2.9 bitcast_dynamic-update-slice_fusion.2
  177.2 0.5 fusion.55
  177.7 2.9 bitcast_dynamic-update-slice_fusion.2
  180.6 79.6 %custom-call.4 = f32[8,128,128]{1,2,0:T(8,128)S(1)} custom-call(f32[8,128,128]{2,1,0:T(8,128)} %get-tuple-element.11), custom_call_target="InvertDiagBlocksLowerTriangular" | custom-call | tf_op jit(solution)/shard_map/jit(_solve_triangular)/triangular_solve | solution.py:8
  260.2 1.5 fusion.18
  261.8 1.6 convolution_subtract_fusion.4
  263.4 0.4 fusion.25
  263.8 2.0 convolution_subtract_fusion.3
  265.8 0.4 fusion.26
  266.2 2.4 convolution_subtract_fusion.6
  268.6 0.4 fusion.27
  268.9 2.8 convolution_subtract_fusion.7
  271.7 0.4 constant_dynamic-update-slice_fusion.12
  272.2 3.2 convolution_subtract_fusion.2
  275.4 0.4 constant_dynamic-update-slice_fusion.18
  276.0 3.6 %convolution_subtract_fusion.5 = f32[128,512]{0,1:T(8,128)S(1)} fusion(f32[768,512]{1,0:T(8,128)S(1)} %constant_dynamic-update-slice_fusion.13, f32[1024,1024]{1,0:T(8,128)} %get-tuple-element.82, f32[1024,512]{0,1:T(8,128)S(1)} %bitcast.66), kind=kOutput, calls=%fused_computation.11 | convolution fusion | flops 604045312 | bytes 2490368 | tf_op jit(solution)/shard_map/jit(_solve_triangular)/triangular_solve | solution.py:8
  279.6 0.4 constant_dynamic-update-slice_fusion.25
  280.1 4.3 %convolution_subtract_fusion.1 = f32[128,512]{0,1:T(8,128)S(1)} fusion(f32[896,512]{1,0:T(8,128)S(1)} %constant_dynamic-update-slice_fusion.19, f32[1024,1024]{1,0:T(8,128)} %get-tuple-element.82, f32[1024,512]{0,1:T(8,128)S(1)} %bitcast.67), kind=kOutput, calls=%fused_computation.7 | convolution fusion | flops 704708608 | bytes 2818048 | tf_op jit(solution)/shard_map/jit(_solve_triangular)/triangular_solve | solution.py:8
  284.4 1.3 convolution_dynamic-update-slice_fusion
  285.9 2.0 fusion.35
  288.0 3.5 %fusion.36 = f32[1024,512]{0,1:T(8,128)S(1)} fusion(f32[1024,512]{1,0:T(8,128)S(1)} %constant_dynamic-update-slice_fusion.26, f32[512,512]{1,0:T(8,128)S(1)} %copy-done), kind=kOutput, calls=%fused_computation.97 | convolution fusion | flops 3221225472 | bytes 5242880 | tf_op jit(solution)/shard_map/rk,rc->kc/dot_general | solution.py:45
  291.5 2.0 pad_maximum_fusion
  293.5 1.1 copy.12
  294.6 1.0 copy.13
  295.7 0.8 dynamic-slice_bitcast_fusion
  296.5 2.0 copy.14
  298.5 6.5 %convolution_subtract_fusion = f32[512,512]{1,0:T(8,128)} fusion(f32[512,512]{1,0:T(8,128)} %param.13, f32[1024,512]{1,0:T(8,128)S(1)} %constant_dynamic-update-slice_fusion.26, f32[1024,512]{1,0:T(8,128)} %all-gather.8.cloned.1.call-done), kind=kOutput, calls=%fused_computation.5 | convolution fusion | flops 3221487616 | bytes 6291456 | tf_op jit(solution)/shard_map/dot_general | solution.py:36
  305.1 32.0 %reduce-scatter.2.cloned.1.call-done = f32[128,768]{0,1:T(8,128)} async-done(((f32[1024,768]{0,1:T(8,128)}), f32[128,768]{0,1:T(8,128)}) %reduce-scatter.2.cloned.1.call-update) | async-done | bytes 393232 | tf_op jit(solution)/shard_map/reduce_scatter | solution.py:46
  337.0 1.0 slice_subtract_fusion
  338.0 0.8 copy.15
  338.8 1.0 fusion.22
  339.9 0.8 copy.16
  (53 shorter events, 1.3 us)
Async XLA Ops:
  7.2 280.8 %copy-start = (f32[512,512]{1,0:T(8,128)S(1)}, f32[512,512]{1,0:T(8,128)}, u32[]{:S(2)}) copy-start(f32[512,512]{1,0:T(8,128)} %param.10) | copy-start | bytes 3145732
  7.2 28.8 %all-gather.4.cloned.1.call-start = ((), (), s32[]{:S(2)}) async-start(), calls=%async_computation.1 | async-start | bytes 1179648 | tf_op jit(solution)/shard_map/all_gather | solution.py:25
  7.9 252.3 %all-gather.6.cloned.1.call-start = ((), (), s32[]{:S(2)}) async-start(), calls=%async_computation.2 | async-start | bytes 2621440 | tf_op jit(solution)/shard_map/all_gather | solution.py:32
  8.7 289.9 %all-gather.8.cloned.1.call-start = ((), (), s32[]{:S(2)}) async-start(), calls=%async_computation.3 | async-start | bytes 2359296 | tf_op jit(solution)/shard_map/all_gather | solution.py:38
  36.0 41.6 %collective-permute-start = (f32[1024,256]{1,0:T(8,128)}, f32[1024,256]{1,0:T(8,128)S(1)}, u32[]{:S(2)}, u32[]{:S(2)}) collective-permute-start(f32[1024,256]{1,0:T(8,128)} %all-gather.4.cloned.1.call-done), channel_id=1, source_target_pairs={{0,1},{1,2},{2,3},{3,0},{4,5},{5,6},{6,7},{7,4},{8,9},{9,10},{10,1... | collective-permute-start | bytes 3145736 | tf_op jit(solution)/shard_map/ppermute | solution.py:28
  77.6 42.2 %collective-permute-start.1 = (f32[1024,256]{1,0:T(8,128)S(1)}, f32[1024,256]{1,0:T(8,128)S(1)}, u32[]{:S(2)}, u32[]{:S(2)}) collective-permute-start(f32[1024,256]{1,0:T(8,128)S(1)} %collective-permute-done), channel_id=1, source_target_pairs={{0,1},{1,2},{2,3},{3,0},{4,5},{5,6},{6,7},{7,4},{8,9},{9,10},{10,1... | collective-permute-start | bytes 3145736 | tf_op jit(solution)/shard_map/ppermute | solution.py:28
  119.8 25.6 %collective-permute-start.2 = (f32[1024,256]{1,0:T(8,128)S(1)}, f32[1024,256]{1,0:T(8,128)}, u32[]{:S(2)}, u32[]{:S(2)}) collective-permute-start(f32[1024,256]{1,0:T(8,128)S(1)} %collective-permute-done.1), channel_id=1, source_target_pairs={{0,1},{1,2},{2,3},{3,0},{4,5},{5,6},{6,7},{7,4},{8,9},{9,10},{10,1... | collective-permute-start | bytes 3145736 | tf_op jit(solution)/shard_map/ppermute | solution.py:28
  119.8 217.2 %reduce-scatter.2.cloned.1.call-start = ((), (), s32[]{:S(2)}) async-start(), calls=%async_computation.4 | async-start | bytes 3538944 | tf_op jit(solution)/shard_map/reduce_scatter | solution.py:46
  146.8 1.3 copy-start.1
  260.2 19.4 %copy-start.4 = (f32[8,128,128]{1,2,0:T(8,128)}, f32[8,128,128]{1,2,0:T(8,128)S(1)}, u32[]{:S(2)}) copy-start(f32[8,128,128]{1,2,0:T(8,128)S(1)} %custom-call.4) | copy-start | bytes 1572868
  260.2 5.9 %copy-start.2 = (f32[512,1024]{1,0:T(8,128)S(1)}, f32[512,1024]{1,0:T(8,128)}, u32[]{:S(2)}) copy-start(f32[512,1024]{1,0:T(8,128)} %all-gather.6.cloned.1.call-done) | copy-start | bytes 6291460
  284.4 1.5 copy-start.3
Sparse Core Ops, SparseCore 0:
  9.9 26.0 all-gather.3
  37.6 63.3 all-gather.5
  119.9 28.2 all-gather.7
  293.7 43.3 reduce-scatter.1
